TPU v7x, 256 devices: a whole 4x4x8 slice. The times are simulated.
256 devices in a mesh: camp: 16 (over z_hi, y, core), hour: 16 (over x, z_lo).
Axes of the slice: x: 4, y: 4, z: 8 (z_hi: 2, z_lo: 4; z = z_hi * 4 + z_lo), core: 2. Of those that a mesh axis runs over, the one named last changes fastest.
Arguments:
- observed: bfloat16 [2048, 2048, 128], P('camp', 'hour'), may hold values from -6 to 6
- bucket: int32 [2048, 2048, 128], P('camp', 'hour'), may hold values from 0 to 8
- propensity: float32 [8], replicated, may hold values from 0.1 to 1
- camp_factor: float32 [2048, 256], P(('camp', 'hour')), may hold values from -2.4 to 2.4
- camp_moment: float32 [2048, 256], P(('camp', 'hour')), may hold values from -0.6 to 0.6
- camp_second: float32 [2048, 256], P(('camp', 'hour')), may hold values from 0.02 to 0.5
- hour_factor: float32 [2048, 256], P(('hour', 'camp')), may hold values from -2.4 to 2.4
- hour_moment: float32 [2048, 256], P(('hour', 'camp')), may hold values from -0.6 to 0.6
- hour_second: float32 [2048, 256], P(('hour', 'camp')), may hold values from 0.02 to 0.5
- delay_factor: float32 [128, 256], replicated, may hold values from -2.4 to 2.4
- delay_moment: float32 [128, 256], replicated, may hold values from -0.6 to 0.6
- delay_second: float32 [128, 256], replicated, may hold values from 0.02 to 0.5
Outputs:
- new_camp: float32 [2048, 256], P(('camp', 'hour'))
- new_hour: float32 [2048, 256], P(('hour', 'camp'))
- new_delay: float32 [128, 256], replicated
Inputs may be any that keep to these rules, and one draw needn't show every extreme that they name: 0 marks a censored entry; bucket b of 1 to 8 takes propensity entry b - 1.
All inputs are finite; a program needn't handle non-finite values.
Results may differ from a plain program's by a relative error of at most 0.01.
Values may be sent and summed in bfloat16 or wider, within the bound.
A program may use at most 128 MiB of HBM per device.

v0:
```python
import math

import jax
import jax.numpy as jnp
from jax import lax
from jax.sharding import PartitionSpec as P

STEPS = 2


learn_rate = 0.1
beta_first = 0.9
beta_second = 0.999
adam_eps = 1e-08


def joined_along(pieces, dim):
    pieces = jnp.moveaxis(pieces, 0, dim)
    shape = pieces.shape
    return pieces.reshape(*shape[:dim], shape[dim] * shape[dim + 1], *shape[dim + 2 :])


def copy_for_each(x, axis):
    copies = jnp.broadcast_to(x, (lax.axis_size(axis), *x.shape))
    return lax.all_to_all(copies, axis, split_axis=0, concat_axis=0, tiled=True)


def gathered_copies(x, axis, dim):
    return joined_along(copy_for_each(x, axis), dim)


def cut_along(x, dim, peers):
    shape = x.shape
    pieces = x.reshape(*shape[:dim], peers, shape[dim] // peers, *shape[dim + 1 :])
    return jnp.moveaxis(pieces, dim, 0)


def summed_on_arrival(x, axis, dim):
    pieces = cut_along(x, dim, lax.axis_size(axis))
    arrived = lax.all_to_all(pieces, axis, split_axis=0, concat_axis=0, tiled=True)
    return arrived.astype(jnp.float32).sum(axis=0)


def of_everyone(x, axis):
    everything = copy_for_each(x, axis)
    return jnp.sum(everything, axis=0)


def adam_update(factor, moment, second, gradient, grad_scale):
    scaled = gradient * grad_scale
    moment = beta_first * moment + (1.0 - beta_first) * scaled
    second = beta_second * second + (1.0 - beta_second) * scaled * scaled
    factor = factor - learn_rate * moment / (jnp.sqrt(second) + adam_eps)
    return (factor, moment, second)


def entry_weights(bucket, propensity):
    inverse = 1.0 / propensity
    weight = jnp.zeros(bucket.shape, jnp.float32)
    for bucket_level in range(propensity.shape[0]):
        weight = weight + jnp.where(
            bucket == bucket_level + 1, inverse[bucket_level], jnp.float32(0.0)
        )
    return weight


def local_terms(observed, weight, camp_block, hour_block, delay_block):
    tile_rows, tile_cols, delay_count = observed.shape
    rank_width = camp_block.shape[1]
    khatri = (
        hour_block.astype(jnp.float32)[:, None, :] * delay_block.astype(jnp.float32)[None, :, :]
    ).astype(jnp.bfloat16)
    khatri = khatri.reshape(tile_cols * delay_count, rank_width)
    model_tile = lax.dot_general(
        camp_block, khatri, (((1,), (1,)), ((), ())), preferred_element_type=jnp.float32
    )
    flat_obs = observed.reshape(tile_rows, tile_cols * delay_count).astype(jnp.float32)
    flat_weight = weight.reshape(tile_rows, tile_cols * delay_count)
    residual = (flat_weight * (model_tile - flat_obs)).astype(jnp.bfloat16)
    spread = lax.dot_general(
        residual, camp_block, (((0,), (0,)), ((), ())), preferred_element_type=jnp.float32
    )
    spread = spread.reshape(tile_cols, delay_count, rank_width)
    hour_grad = jnp.sum(spread * delay_block.astype(jnp.float32)[None, :, :], axis=1)
    delay_grad = jnp.sum(spread * hour_block.astype(jnp.float32)[:, None, :], axis=0)
    return (khatri, residual, hour_grad, delay_grad)


def body(
    observed,
    bucket,
    propensity,
    camp_factor,
    camp_moment,
    camp_second,
    hour_factor,
    hour_moment,
    hour_second,
    delay_factor,
    delay_moment,
    delay_second,
):
    tile_rows, tile_cols, delay_count = observed.shape
    camp_count = lax.axis_size("camp")
    hour_count = lax.axis_size("hour")
    campaigns = tile_rows * camp_count
    total_hours = tile_cols * hour_count
    camp_scale = 1.0 / math.sqrt(total_hours * delay_count)
    hour_scale = 1.0 / math.sqrt(campaigns * delay_count)
    delay_scale = 1.0 / math.sqrt(campaigns * total_hours)
    weight = entry_weights(bucket, propensity)
    delay_share = delay_count // hour_count
    offset = lax.axis_index("hour") * delay_share
    delay_own = lax.dynamic_slice_in_dim(delay_factor, offset, delay_share, 0)
    delay_moment = lax.dynamic_slice_in_dim(delay_moment, offset, delay_share, 0)
    delay_second = lax.dynamic_slice_in_dim(delay_second, offset, delay_share, 0)
    for iteration in range(STEPS):
        camp_block = gathered_copies(camp_factor.astype(jnp.bfloat16), "hour", 0)
        hour_block = gathered_copies(hour_factor.astype(jnp.bfloat16), "camp", 0)
        delay_block = delay_factor.astype(jnp.bfloat16)
        khatri, residual, hour_grad, delay_grad = local_terms(
            observed, weight, camp_block, hour_block, delay_block
        )
        camp_grad = summed_on_arrival(
            jnp.dot(residual, khatri, preferred_element_type=jnp.float32).astype(jnp.bfloat16),
            "hour",
            0,
        )
        hour_grad = summed_on_arrival(hour_grad.astype(jnp.bfloat16), "camp", 0)
        camp_factor, camp_moment, camp_second = adam_update(
            camp_factor, camp_moment, camp_second, camp_grad, camp_scale
        )
        hour_factor, hour_moment, hour_second = adam_update(
            hour_factor, hour_moment, hour_second, hour_grad, hour_scale
        )
        delay_grad = summed_on_arrival(delay_grad.astype(jnp.bfloat16), "hour", 0)
        delay_grad = of_everyone(delay_grad, "camp")
        delay_own, delay_moment, delay_second = adam_update(
            delay_own, delay_moment, delay_second, delay_grad, delay_scale
        )
        delay_factor = gathered_copies(delay_own, "hour", 0)
    return (camp_factor, hour_factor, delay_factor)


def solution(mesh):
    in_specs = (
        P("camp", "hour", None),
        P("camp", "hour", None),
        P(),
        P(("camp", "hour"), None),
        P(("camp", "hour"), None),
        P(("camp", "hour"), None),
        P(("hour", "camp"), None),
        P(("hour", "camp"), None),
        P(("hour", "camp"), None),
        P(),
        P(),
        P(),
    )
    out_specs = (P(("camp", "hour"), None), P(("hour", "camp"), None), P())
    return jax.shard_map(body, mesh=mesh, in_specs=in_specs, out_specs=out_specs, check_vma=False)
```

profile of v0, /device:TPU:1, one launch (start us, length us, event | category | flops | bytes accessed | tf_op | source)
XLA Modules:
  0.0 262.5 jit_solution(2979683713364399185)
XLA Ops:
  2.0 12.6 %all-to-all-start = ((bf16[16,8,256]{2,1,0:T(8,128)(2,1)}), bf16[16,8,256]{2,1,0:T(8,128)(2,1)S(1)}, u32[]{:S(2)}, u32[]{:S(2)}) async-start(bf16[16,8,256]{2,1,0:T(8,128)(2,1)} %broadcast_in_dim.77), calls=%async_computation | async-start | bytes 131072 | tf_op jit(solution)/shard_map/all_to_all | solution.py:25
  16.6 15.2 %select_add_fusion = f32[128,128,128]{2,1,0:T(8,128)} fusion(s32[128,128,128]{2,1,0:T(8,128)} %param.13, f32[]{:T(128)} %bitcast.7, f32[]{:T(128)} %bitcast.6, f32[]{:T(128)} %bitcast.5, f32[]{:T(128)} %bitcast.4, f32[]{:T(128)} %bitcast.3, f32[]{:T(128)} %bitcast.2, f32[]{:T(128)} %bitcast.1, f32[]{:T(128)} %bitcast), kind=kLoop, calls=%fused_computation.13 | loop fusion | flops 48234496 | bytes 16777248 | tf_op jit(solution)/shard_map/add | solution.py:61
  31.9 9.3 %copy.18 = f32[128,128,128]{0,2,1:T(8,128)} copy(f32[128,128,128]{2,1,0:T(8,128)} %select_add_fusion) | data formatting | bytes 16777216 | tf_op jit(solution)/shard_map/add | solution.py:61
  41.2 7.7 %copy.19 = f32[128,128,128]{0,2,1:T(8,128)} copy(bf16[128,128,128]{2,1,0:T(8,128)(2,1)} %param.12) | data formatting | bytes 12582912 | tf_op jit(solution)/shard_map/convert_element_type | solution.py:77
  49.5 5.5 %all-to-all-start.1 = ((bf16[16,8,256]{2,1,0:T(8,128)(2,1)}), bf16[16,8,256]{2,1,0:T(8,128)(2,1)S(1)}, u32[]{:S(2)}, u32[]{:S(2)}) async-start(bf16[16,8,256]{2,1,0:T(8,128)(2,1)} %broadcast_in_dim.78), calls=%async_computation.1 | async-start | bytes 131072 | tf_op jit(solution)/shard_map/all_to_all | solution.py:25
  55.1 6.7 %multiply_convert_fusion.1 = bf16[128,128,256]{2,1,0:T(8,128)(2,1)} fusion(f32[128,256]{1,0:T(8,128)S(1)} %convert_convert_fusion, f32[128,256]{1,0:T(8,128)S(1)} %bitcast_convert_fusion.2), kind=kLoop, calls=%fused_computation.12 | loop fusion | flops 8388608 | bytes 8650752 | tf_op jit(solution)/shard_map/convert_element_type | solution.py:72
  62.1 10.5 %fusion.3 = bf16[128,16384]{0,1:T(8,128)(2,1)S(1)} fusion(f32[128,16384]{0,1:T(8,128)} %bitcast.82, f32[128,16384]{0,1:T(8,128)} %bitcast.84, bf16[16384,256]{1,0:T(8,128)(2,1)} %bitcast.80, bf16[16,8,256]{2,1,0:T(8,128)(2,1)S(1)} %all-to-all-done.1), kind=kOutput, calls=%fused_computation.5 | convolution fusion | flops 1080033280 | bytes 29425664 | tf_op jit(solution)/shard_map/dot_general | solution.py:74
  72.6 4.2 %multiply_reduce_fusion.3 = (bf16[128,256]{1,0:T(8,128)(2,1)}, bf16[128,256]{1,0:T(8,128)(2,1)}) fusion(f32[128,256]{1,0:T(8,128)S(1)} %convert_convert_fusion, f32[128,256]{1,0:T(8,128)S(1)} %bitcast_convert_fusion.2, bf16[128,128,128]{2,1,0:T(8,128)(2,1)S(1)} %bitcast.87, bf16[16,8,256]{2,1,0:T(8,128)(2,1)S(1)} %all-to-all-done.1), kind=kOutput, calls=%fused_computation.11 | convolution fusion | flops 1090453504 | bytes 4653056 | tf_op jit(solution)/shard_map/dot_general | solution.py:80
  76.8 11.0 %all-to-all-start.4 = ((bf16[16,8,256]{2,1,0:T(8,128)(2,1)}), bf16[16,8,256]{2,1,0:T(8,128)(2,1)S(1)}, u32[]{:S(2)}, u32[]{:S(2)}) async-start(bf16[16,8,256]{2,1,0:T(8,128)(2,1)} %bitcast.65), calls=%async_computation.4 | async-start | bytes 131072 | tf_op jit(solution)/shard_map/all_to_all | solution.py:40
  87.8 9.7 %all-to-all-done.4 = bf16[16,8,256]{2,1,0:T(8,128)(2,1)S(1)} async-done(((bf16[16,8,256]{2,1,0:T(8,128)(2,1)}), bf16[16,8,256]{2,1,0:T(8,128)(2,1)S(1)}, u32[]{:S(2)}, u32[]{:S(2)}) %all-to-all-start.4) | async-done | bytes 65568 | tf_op jit(solution)/shard_map/all_to_all | solution.py:40
  97.5 5.8 %all-to-all-start.6 = ((bf16[16,8,256]{2,1,0:T(8,128)(2,1)}), bf16[16,8,256]{2,1,0:T(8,128)(2,1)S(1)}, u32[]{:S(2)}, u32[]{:S(2)}) async-start(bf16[16,8,256]{2,1,0:T(8,128)(2,1)} %bitcast.64), calls=%async_computation.6 | async-start | bytes 131072 | tf_op jit(solution)/shard_map/all_to_all | solution.py:40
  103.4 7.1 %fusion.5 = bf16[16,8,256]{2,1,0:T(8,128)(2,1)} fusion(bf16[128,16384]{0,1:T(8,128)(2,1)} %copy-done.1, bf16[16384,256]{1,0:T(8,128)(2,1)} %bitcast.81), kind=kOutput, calls=%fused_computation.16 | convolution fusion | flops 1073774592 | bytes 12648448 | tf_op jit(solution)/shard_map/dot_general | solution.py:125
  110.5 7.0 %all-to-all-start.2 = ((bf16[16,8,256]{2,1,0:T(8,128)(2,1)}), bf16[16,8,256]{2,1,0:T(8,128)(2,1)S(1)}, u32[]{:S(2)}, u32[]{:S(2)}) async-start(bf16[16,8,256]{2,1,0:T(8,128)(2,1)} %fusion.5), calls=%async_computation.2 | async-start | bytes 131072 | tf_op jit(solution)/shard_map/all_to_all | solution.py:40
  117.5 6.9 %all-to-all-done.2 = bf16[16,8,256]{2,1,0:T(8,128)(2,1)S(1)} async-done(((bf16[16,8,256]{2,1,0:T(8,128)(2,1)}), bf16[16,8,256]{2,1,0:T(8,128)(2,1)S(1)}, u32[]{:S(2)}, u32[]{:S(2)}) %all-to-all-start.2) | async-done | bytes 65568 | tf_op jit(solution)/shard_map/all_to_all | solution.py:40
  125.1 5.7 %all-to-all-start.7 = ((f32[16,8,256]{2,1,0:T(8,128)}), f32[16,8,256]{2,1,0:T(8,128)S(1)}, u32[]{:S(2)}, u32[]{:S(2)}) async-start(f32[16,8,256]{2,1,0:T(8,128)} %broadcast_in_dim.81), calls=%async_computation.7 | async-start | bytes 262144 | tf_op jit(solution)/shard_map/all_to_all | solution.py:25
  130.9 10.0 %all-to-all-done.7 = f32[16,8,256]{2,1,0:T(8,128)S(1)} async-done(((f32[16,8,256]{2,1,0:T(8,128)}), f32[16,8,256]{2,1,0:T(8,128)S(1)}, u32[]{:S(2)}, u32[]{:S(2)}) %all-to-all-start.7) | async-done | bytes 131104 | tf_op jit(solution)/shard_map/all_to_all | solution.py:25
  141.6 4.0 %all-to-all-start.5 = ((bf16[16,8,256]{2,1,0:T(8,128)(2,1)}), bf16[16,8,256]{2,1,0:T(8,128)(2,1)S(1)}, u32[]{:S(2)}, u32[]{:S(2)}) async-start(bf16[16,8,256]{2,1,0:T(8,128)(2,1)} %broadcast_in_dim.80), calls=%async_computation.5 | async-start | bytes 131072 | tf_op jit(solution)/shard_map/all_to_all | solution.py:25
  146.3 9.0 %all-to-all-done.5 = bf16[16,8,256]{2,1,0:T(8,128)(2,1)S(1)} async-done(((bf16[16,8,256]{2,1,0:T(8,128)(2,1)}), bf16[16,8,256]{2,1,0:T(8,128)(2,1)S(1)}, u32[]{:S(2)}, u32[]{:S(2)}) %all-to-all-start.5) | async-done | bytes 65568 | tf_op jit(solution)/shard_map/all_to_all | solution.py:25
  156.0 3.5 %all-to-all-start.8 = ((bf16[16,8,256]{2,1,0:T(8,128)(2,1)}), bf16[16,8,256]{2,1,0:T(8,128)(2,1)S(1)}, u32[]{:S(2)}, u32[]{:S(2)}) async-start(bf16[16,8,256]{2,1,0:T(8,128)(2,1)} %broadcast_in_dim.82), calls=%async_computation.8 | async-start | bytes 131072 | tf_op jit(solution)/shard_map/all_to_all | solution.py:25
  159.5 7.0 %all-to-all-done.8 = bf16[16,8,256]{2,1,0:T(8,128)(2,1)S(1)} async-done(((bf16[16,8,256]{2,1,0:T(8,128)(2,1)}), bf16[16,8,256]{2,1,0:T(8,128)(2,1)S(1)}, u32[]{:S(2)}, u32[]{:S(2)}) %all-to-all-start.8) | async-done | bytes 65568 | tf_op jit(solution)/shard_map/all_to_all | solution.py:25
  170.6 6.7 %multiply_convert_fusion = bf16[128,128,256]{2,1,0:T(8,128)(2,1)} fusion(f32[128,256]{1,0:T(8,128)S(1)} %bitcast_convert_fusion, f32[128,256]{1,0:T(8,128)S(1)} %bitcast_convert_fusion.1), kind=kLoop, calls=%fused_computation.9 | loop fusion | flops 8388608 | bytes 8650752 | tf_op jit(solution)/shard_map/convert_element_type | solution.py:72
  177.6 10.5 %fusion.4 = bf16[128,16384]{0,1:T(8,128)(2,1)S(1)} fusion(f32[128,16384]{0,1:T(8,128)} %bitcast.83, f32[128,16384]{0,1:T(8,128)} %bitcast.85, bf16[16384,256]{1,0:T(8,128)(2,1)} %bitcast.78, bf16[16,8,256]{2,1,0:T(8,128)(2,1)S(1)} %all-to-all-done.3), kind=kOutput, calls=%fused_computation.6 | convolution fusion | flops 1080033280 | bytes 29425664 | tf_op jit(solution)/shard_map/dot_general | solution.py:74
  188.1 4.0 %multiply_reduce_fusion = (bf16[128,256]{1,0:T(8,128)(2,1)S(1)}, bf16[128,256]{1,0:T(8,128)(2,1)}) fusion(f32[128,256]{1,0:T(8,128)S(1)} %bitcast_convert_fusion.1, f32[128,256]{1,0:T(8,128)S(1)} %bitcast_convert_fusion, bf16[128,128,128]{2,1,0:T(8,128)(2,1)S(1)} %bitcast.86, bf16[16,8,256]{2,1,0:T(8,128)(2,1)S(1)} %all-to-all-done.3), kind=kOutput, calls=%fused_computation.7 | convolution fusion | flops 1090453504 | bytes 4653056 | tf_op jit(solution)/shard_map/dot_general | solution.py:80
  192.1 13.5 %all_to_all.70 = bf16[16,8,256]{2,1,0:T(8,128)(2,1)S(1)} all-to-all(bf16[16,8,256]{2,1,0:T(8,128)(2,1)S(1)} %bitcast.89), channel_id=1, replica_groups=mesh['camp'=16,'hour'=16] {'hour'}, dimensions={0} | all-to-all | bytes 131072 | tf_op jit(solution)/shard_map/all_to_all | solution.py:40
  205.6 6.8 %all-to-all-start.10 = ((bf16[16,8,256]{2,1,0:T(8,128)(2,1)}), bf16[16,8,256]{2,1,0:T(8,128)(2,1)S(1)}, u32[]{:S(2)}, u32[]{:S(2)}) async-start(bf16[16,8,256]{2,1,0:T(8,128)(2,1)} %bitcast.63), calls=%async_computation.10 | async-start | bytes 131072 | tf_op jit(solution)/shard_map/all_to_all | solution.py:40
  212.4 7.1 %fusion.6 = bf16[16,8,256]{2,1,0:T(8,128)(2,1)} fusion(bf16[128,16384]{0,1:T(8,128)(2,1)} %copy-done, bf16[16384,256]{1,0:T(8,128)(2,1)} %bitcast.79), kind=kOutput, calls=%fused_computation.17 | convolution fusion | flops 1073774592 | bytes 12648448 | tf_op jit(solution)/shard_map/dot_general | solution.py:125
  222.9 7.0 %all-to-all-start.12 = ((f32[16,8,256]{2,1,0:T(8,128)}), f32[16,8,256]{2,1,0:T(8,128)S(1)}, u32[]{:S(2)}, u32[]{:S(2)}) async-start(f32[16,8,256]{2,1,0:T(8,128)} %broadcast_in_dim.83), calls=%async_computation.12 | async-start | bytes 262144 | tf_op jit(solution)/shard_map/all_to_all | solution.py:25
  230.5 9.4 %all-to-all-done.12 = f32[16,8,256]{2,1,0:T(8,128)S(1)} async-done(((f32[16,8,256]{2,1,0:T(8,128)}), f32[16,8,256]{2,1,0:T(8,128)S(1)}, u32[]{:S(2)}, u32[]{:S(2)}) %all-to-all-start.12) | async-done | bytes 131104 | tf_op jit(solution)/shard_map/all_to_all | solution.py:25
  239.9 3.5 %all-to-all-start.9 = ((bf16[16,8,256]{2,1,0:T(8,128)(2,1)}), bf16[16,8,256]{2,1,0:T(8,128)(2,1)S(1)}, u32[]{:S(2)}, u32[]{:S(2)}) async-start(bf16[16,8,256]{2,1,0:T(8,128)(2,1)} %fusion.6), calls=%async_computation.9 | async-start | bytes 131072 | tf_op jit(solution)/shard_map/all_to_all | solution.py:40
  244.2 6.2 %all-to-all-done.9 = bf16[16,8,256]{2,1,0:T(8,128)(2,1)S(1)} async-done(((bf16[16,8,256]{2,1,0:T(8,128)(2,1)}), bf16[16,8,256]{2,1,0:T(8,128)(2,1)S(1)}, u32[]{:S(2)}, u32[]{:S(2)}) %all-to-all-start.9) | async-done | bytes 65568 | tf_op jit(solution)/shard_map/all_to_all | solution.py:40
  251.1 3.5 %all-to-all-start.13 = ((f32[16,8,256]{2,1,0:T(8,128)}), f32[16,8,256]{2,1,0:T(8,128)S(1)}, u32[]{:S(2)}, u32[]{:S(2)}) async-start(f32[16,8,256]{2,1,0:T(8,128)} %broadcast_in_dim.84), calls=%async_computation.13 | async-start | bytes 262144 | tf_op jit(solution)/shard_map/all_to_all | solution.py:25
  255.2 6.6 %all-to-all-done.13 = f32[16,8,256]{2,1,0:T(8,128)S(1)} async-done(((f32[16,8,256]{2,1,0:T(8,128)}), f32[16,8,256]{2,1,0:T(8,128)S(1)}, u32[]{:S(2)}, u32[]{:S(2)}) %all-to-all-start.13) | async-done | bytes 131104 | tf_op jit(solution)/shard_map/all_to_all | solution.py:25
  (55 shorter events, 18.4 us)
Async XLA Ops:
  2.0 46.9 %all-to-all-start = ((bf16[16,8,256]{2,1,0:T(8,128)(2,1)}), bf16[16,8,256]{2,1,0:T(8,128)(2,1)S(1)}, u32[]{:S(2)}, u32[]{:S(2)}) async-start(bf16[16,8,256]{2,1,0:T(8,128)(2,1)} %broadcast_in_dim.77), calls=%async_computation | async-start | bytes 131072 | tf_op jit(solution)/shard_map/all_to_all | solution.py:25
  41.2 7.7 %copy-start.2 = (f32[128,256]{1,0:T(8,128)S(1)}, f32[128,256]{1,0:T(8,128)}, u32[]{:S(2)}) copy-start(f32[128,256]{1,0:T(8,128)} %param.21) | copy-start | bytes 393220
  49.5 12.5 %all-to-all-start.1 = ((bf16[16,8,256]{2,1,0:T(8,128)(2,1)}), bf16[16,8,256]{2,1,0:T(8,128)(2,1)S(1)}, u32[]{:S(2)}, u32[]{:S(2)}) async-start(bf16[16,8,256]{2,1,0:T(8,128)(2,1)} %broadcast_in_dim.78), calls=%async_computation.1 | async-start | bytes 131072 | tf_op jit(solution)/shard_map/all_to_all | solution.py:25
  72.6 4.2 %copy-start.1 = (bf16[128,16384]{0,1:T(8,128)(2,1)}, bf16[128,16384]{0,1:T(8,128)(2,1)S(1)}, u32[]{:S(2)}) copy-start(bf16[128,16384]{0,1:T(8,128)(2,1)S(1)} %fusion.3) | copy-start | bytes 12582916
  76.8 20.7 %all-to-all-start.4 = ((bf16[16,8,256]{2,1,0:T(8,128)(2,1)}), bf16[16,8,256]{2,1,0:T(8,128)(2,1)S(1)}, u32[]{:S(2)}, u32[]{:S(2)}) async-start(bf16[16,8,256]{2,1,0:T(8,128)(2,1)} %bitcast.65), calls=%async_computation.4 | async-start | bytes 131072 | tf_op jit(solution)/shard_map/all_to_all | solution.py:40
  97.5 13.0 %all-to-all-start.6 = ((bf16[16,8,256]{2,1,0:T(8,128)(2,1)}), bf16[16,8,256]{2,1,0:T(8,128)(2,1)S(1)}, u32[]{:S(2)}, u32[]{:S(2)}) async-start(bf16[16,8,256]{2,1,0:T(8,128)(2,1)} %bitcast.64), calls=%async_computation.6 | async-start | bytes 131072 | tf_op jit(solution)/shard_map/all_to_all | solution.py:40
  103.3 14.2 %copy-start.3 = (f32[8,256]{1,0:T(8,128)S(1)}, f32[8,256]{1,0:T(8,128)}, u32[]{:S(2)}) copy-start(f32[8,256]{1,0:T(8,128)} %param.18) | copy-start | bytes 24580
  103.3 14.2 %copy-start.5 = (f32[8,256]{1,0:T(8,128)S(1)}, f32[8,256]{1,0:T(8,128)}, u32[]{:S(2)}) copy-start(f32[8,256]{1,0:T(8,128)} %param.20) | copy-start | bytes 24580
  103.3 14.2 %copy-start.6 = (f32[8,256]{1,0:T(8,128)S(1)}, f32[8,256]{1,0:T(8,128)}, u32[]{:S(2)}) copy-start(f32[8,256]{1,0:T(8,128)} %param.19) | copy-start | bytes 24580
  103.3 27.5 %copy-start.4 = (f32[8,256]{1,0:T(8,128)S(1)}, f32[8,256]{1,0:T(8,128)}, u32[]{:S(2)}) copy-start(f32[8,256]{1,0:T(8,128)} %param.15) | copy-start | bytes 24580
  103.3 27.5 %copy-start.7 = (f32[8,256]{1,0:T(8,128)S(1)}, f32[8,256]{1,0:T(8,128)}, u32[]{:S(2)}) copy-start(f32[8,256]{1,0:T(8,128)} %param.17) | copy-start | bytes 24580
  103.4 27.5 %copy-start.8 = (f32[8,256]{1,0:T(8,128)S(1)}, f32[8,256]{1,0:T(8,128)}, u32[]{:S(2)}) copy-start(f32[8,256]{1,0:T(8,128)} %param.16) | copy-start | bytes 24580
  110.5 13.9 %all-to-all-start.2 = ((bf16[16,8,256]{2,1,0:T(8,128)(2,1)}), bf16[16,8,256]{2,1,0:T(8,128)(2,1)S(1)}, u32[]{:S(2)}, u32[]{:S(2)}) async-start(bf16[16,8,256]{2,1,0:T(8,128)(2,1)} %fusion.5), calls=%async_computation.2 | async-start | bytes 131072 | tf_op jit(solution)/shard_map/all_to_all | solution.py:40
  125.1 15.8 %all-to-all-start.7 = ((f32[16,8,256]{2,1,0:T(8,128)}), f32[16,8,256]{2,1,0:T(8,128)S(1)}, u32[]{:S(2)}, u32[]{:S(2)}) async-start(f32[16,8,256]{2,1,0:T(8,128)} %broadcast_in_dim.81), calls=%async_computation.7 | async-start | bytes 262144 | tf_op jit(solution)/shard_map/all_to_all | solution.py:25
  141.6 13.8 %all-to-all-start.5 = ((bf16[16,8,256]{2,1,0:T(8,128)(2,1)}), bf16[16,8,256]{2,1,0:T(8,128)(2,1)S(1)}, u32[]{:S(2)}, u32[]{:S(2)}) async-start(bf16[16,8,256]{2,1,0:T(8,128)(2,1)} %broadcast_in_dim.80), calls=%async_computation.5 | async-start | bytes 131072 | tf_op jit(solution)/shard_map/all_to_all | solution.py:25
  156.0 10.5 %all-to-all-start.8 = ((bf16[16,8,256]{2,1,0:T(8,128)(2,1)}), bf16[16,8,256]{2,1,0:T(8,128)(2,1)S(1)}, u32[]{:S(2)}, u32[]{:S(2)}) async-start(bf16[16,8,256]{2,1,0:T(8,128)(2,1)} %broadcast_in_dim.82), calls=%async_computation.8 | async-start | bytes 131072 | tf_op jit(solution)/shard_map/all_to_all | solution.py:25
  167.1 10.4 %all-to-all-start.3 = ((bf16[16,8,256]{2,1,0:T(8,128)(2,1)}), bf16[16,8,256]{2,1,0:T(8,128)(2,1)S(1)}, u32[]{:S(2)}, u32[]{:S(2)}) async-start(bf16[16,8,256]{2,1,0:T(8,128)(2,1)} %broadcast_in_dim.79), calls=%async_computation.3 | async-start | bytes 131072 | tf_op jit(solution)/shard_map/all_to_all | solution.py:25
  188.1 4.1 %copy-start = (bf16[128,16384]{0,1:T(8,128)(2,1)}, bf16[128,16384]{0,1:T(8,128)(2,1)S(1)}, u32[]{:S(2)}) copy-start(bf16[128,16384]{0,1:T(8,128)(2,1)S(1)} %fusion.4) | copy-start | bytes 12582916
  205.6 16.6 %all-to-all-start.10 = ((bf16[16,8,256]{2,1,0:T(8,128)(2,1)}), bf16[16,8,256]{2,1,0:T(8,128)(2,1)S(1)}, u32[]{:S(2)}, u32[]{:S(2)}) async-start(bf16[16,8,256]{2,1,0:T(8,128)(2,1)} %bitcast.63), calls=%async_computation.10 | async-start | bytes 131072 | tf_op jit(solution)/shard_map/all_to_all | solution.py:40
  222.9 17.0 %all-to-all-start.12 = ((f32[16,8,256]{2,1,0:T(8,128)}), f32[16,8,256]{2,1,0:T(8,128)S(1)}, u32[]{:S(2)}, u32[]{:S(2)}) async-start(f32[16,8,256]{2,1,0:T(8,128)} %broadcast_in_dim.83), calls=%async_computation.12 | async-start | bytes 262144 | tf_op jit(solution)/shard_map/all_to_all | solution.py:25
  239.9 10.5 %all-to-all-start.9 = ((bf16[16,8,256]{2,1,0:T(8,128)(2,1)}), bf16[16,8,256]{2,1,0:T(8,128)(2,1)S(1)}, u32[]{:S(2)}, u32[]{:S(2)}) async-start(bf16[16,8,256]{2,1,0:T(8,128)(2,1)} %fusion.6), calls=%async_computation.9 | async-start | bytes 131072 | tf_op jit(solution)/shard_map/all_to_all | solution.py:40
  251.1 10.8 %all-to-all-start.13 = ((f32[16,8,256]{2,1,0:T(8,128)}), f32[16,8,256]{2,1,0:T(8,128)S(1)}, u32[]{:S(2)}, u32[]{:S(2)}) async-start(f32[16,8,256]{2,1,0:T(8,128)} %broadcast_in_dim.84), calls=%async_computation.13 | async-start | bytes 262144 | tf_op jit(solution)/shard_map/all_to_all | solution.py:25
where the time goes:
time: 265 us; the launch traced here: 262 us
  starting transfers between devices  79.4 us (30%)
  waiting for transfers between devices  68.2 us (26%)
  matrix products  43.4 us (16%)
  other arithmetic  33.6 us (13%)
  local copies, waits for them, and re-layouts  23.6 us (9%)
  blocking collectives  13.5 us (5%)
    all_to_all x8, starting transfers between devices, copy_for_each(): return lax.all_to_all(copies, axis, split_axis=0, concat_axis=0, tiled=True)  45.3 us
    all_to_all x8, waiting for transfers between devices, copy_for_each(): return lax.all_to_all(copies, axis, split_axis=0, concat_axis=0, tiled=True)  42.6 us
    all_to_all x5, starting transfers between devices, summed_on_arrival(): lax.all_to_all(pieces, axis, split_axis=0, concat_axis=0, tiled=True)  34.1 us
    all_to_all x5, waiting for transfers between devices, summed_on_arrival(): lax.all_to_all(pieces, axis, split_axis=0, concat_axis=0, tiled=True)  25.6 us
    dot_general x2, matrix products, local_terms(): lax.dot_general(camp_block, khatri, (((1,), (1,)), ((), ())), preferred_e...  21 us
    add x1, other arithmetic, entry_weights(): weight + jnp.where(bucket == bucket_level + 1, inverse[bucket_level], jnp...  15.2 us
    dot_general x2, matrix products, body(): jnp.dot(residual, khatri, preferred_element_type=jnp.float32)  14.2 us
    all_to_all x1, blocking collectives, summed_on_arrival(): lax.all_to_all(pieces, axis, split_axis=0, concat_axis=0, tiled=True)  13.5 us
  transfers between devices with their start and end apart: 13, of which 11 were waited for; matrix products, arithmetic and copies ran while one was open for 25% of the time, Pallas kernels for 0%

commit v1 on v0

v1 whole, which is shorter than its diff:
```python
import functools
import math

import jax
import jax.numpy as jnp
from jax import lax
from jax.experimental import pallas as pl
from jax.experimental.pallas import tpu as pltpu
from jax.sharding import PartitionSpec as P

STEPS = 2

learn_rate = 0.1
beta_first = 0.9
beta_second = 0.999
adam_eps = 1e-08

MESH = pl.DeviceIdType.MESH
f32 = jnp.float32
bf16 = jnp.bfloat16

CHUNKS = 8
ROWS_A, ROWS_B, ROWS_C, GRAD_A, GRAD_B, GRAD_C, SUM_C = range(7)
KINDS = 7


def split_sizes(camp_count, hour_count):
    high, core = 2, 2
    along_y = camp_count // (high * core)
    along_x = 4 if hour_count == 16 else 2
    return high, along_y, core, along_x, hour_count // along_x


def adam_update(factor, moment, second, gradient, grad_scale):
    scaled = gradient * grad_scale
    moment = beta_first * moment + (1.0 - beta_first) * scaled
    second = beta_second * second + (1.0 - beta_second) * scaled * scaled
    factor = factor - learn_rate * moment / (jnp.sqrt(second) + adam_eps)
    return factor, moment, second


def dot(a, b, dims):
    return lax.dot_general(a, b, (dims, ((), ())), preferred_element_type=f32)


def kernel(
    sizes,
    scales,
    obs_hbm,
    bucket_hbm,
    prop_hbm,
    *refs,
):
    state_hbm, refs = refs[:9], refs[9:]
    new_a, new_b, new_c, refs = *refs[:3], refs[3:]
    (
        obs,
        bucket,
        weight,
        prop,
        inverse,
        fa,
        ma,
        va,
        fb,
        mb,
        vb,
        fc,
        mc,
        vc,
        a_own,
        b_own,
        c_own,
        a_all,
        b_all,
        c_all,
        c_last,
        ga_out,
        gb_out,
        gc_out,
        sc_out,
        ga_in,
        gb_in,
        gc_in,
        sc_in,
        a32,
        b16,
        b32,
        c16,
        ct16,
        ga,
        gb,
        gc,
        state_sem,
        chunk_sem,
        send_sem,
        recv_sem,
    ) = refs
    high, along_y, cores, along_x, low = sizes
    n_hour, n_camp = along_x * low, high * along_y * cores
    n_xy, n_cz = along_x * along_y, cores * high * low
    scale_a, scale_b, scale_c = scales
    rows, cols, delays = obs.shape
    rank = a32.shape[1]
    part_a, part_c = rows // n_hour, delays // n_xy

    camp, hour = lax.axis_index("camp"), lax.axis_index("hour")
    z_hi, y, core = camp // (along_y * cores), (camp // cores) % along_y, camp % cores
    x, z_lo = hour // low, hour % low
    xy = x * along_y + y
    cz = (core * high + z_hi) * low + z_lo

    def hour_peer(p):
        return {"camp": camp, "hour": p}

    def camp_peer(p):
        return {"camp": p, "hour": hour}

    def xy_peer(p):
        return {"camp": (z_hi * along_y + p % along_y) * cores + core, "hour": (p // along_y) * low + z_lo}

    def cz_peer(p):
        at = (p // low) % high
        return {"camp": (at * along_y + y) * cores + p // (low * high), "hour": x * low + p % low}

    by_hour = (n_hour, hour, hour_peer)
    by_camp = (n_camp, camp, camp_peer)
    by_xy = (n_xy, xy, xy_peer)
    by_cz = (n_cz, cz, cz_peer)
    groups = (by_hour, by_camp, by_xy, by_cz)

    states = (fa, ma, va, fb, mb, vb, fc, mc, vc)
    loads = [pltpu.make_async_copy(h, v, state_sem.at[i]) for i, (h, v) in enumerate(zip(state_hbm, states))]
    loads.append(pltpu.make_async_copy(prop_hbm, prop, state_sem.at[9]))
    for load in loads:
        load.start()
    chunk = rows // CHUNKS

    def chunks_of(source, target, row):
        ats = [pl.ds(n * chunk, chunk) for n in range(CHUNKS)]
        return [pltpu.make_async_copy(source.at[at], target.at[at], chunk_sem.at[row, n]) for n, at in enumerate(ats)]

    bucket_chunks, obs_chunks = chunks_of(bucket_hbm, bucket, 0), chunks_of(obs_hbm, obs, 1)
    for load in bucket_chunks + obs_chunks:
        load.start()

    barrier = pltpu.get_barrier_semaphore()
    for size, me, peer in groups:

        def greet(t, _, size=size, me=me, peer=peer):
            pl.semaphore_signal(barrier, inc=1, device_id=peer((me + t) % size), device_id_type=MESH)
            return 0

        lax.fori_loop(1, size, greet, 0)
    pl.semaphore_wait(barrier, sum(size - 1 for size, _, _ in groups))

    def send(src, dst, step, kind, device):
        pltpu.make_async_remote_copy(
            src_ref=src,
            dst_ref=dst,
            send_sem=send_sem.at[step, kind],
            recv_sem=recv_sem.at[step, kind],
            device_id=device,
            device_id_type=MESH,
        ).start()

    def to_each(group, src, dst, step, kind):
        size, me, peer = group

        def one(t, _):
            p = (me + t) % size
            block = src.at[step] if len(src.shape) == len(dst.shape) - 1 else src.at[step, p]
            send(block, dst.at[step, me], step, kind, peer(p))
            return 0

        lax.fori_loop(1, size, one, 0)

    def arrived(size, dst, step, kind):
        got = dst.at[step, pl.ds(0, size - 1)]
        pltpu.make_async_copy(got, got, recv_sem.at[step, kind]).wait()

    def total(buf, step, size):
        out = buf[step, 0].astype(f32)
        for p in range(1, size):
            out = out + buf[step, p].astype(f32)
        return out

    def give(own, everyone, group, value, step, kind):
        own[step] = value
        everyone[step, group[1]] = value
        to_each(group, own, everyone, step, kind)

    for load in loads:
        load.wait()
    give(a_own, a_all, by_hour, fa[...].astype(bf16), 0, ROWS_A)
    give(b_own, b_all, by_camp, fb[...].astype(bf16), 0, ROWS_B)

    for level in range(prop.shape[0]):
        inverse[level] = 1.0 / jnp.full((8, delays), prop[level], f32)

    def weigh(i, _):
        b = bucket[i].reshape(cols // 8, 8, delays)

        def inv(level):
            return jnp.broadcast_to(inverse[level][None], b.shape)

        one, two, four = (b & 1) != 0, (b & 2) != 0, (b & 4) != 0
        last = jnp.where(b > 7, inv(7), 0.0)
        low_half = jnp.where(two, jnp.where(one, inv(2), inv(1)), jnp.where(one, inv(0), last))
        high_half = jnp.where(two, jnp.where(one, inv(6), inv(5)), jnp.where(one, inv(4), inv(3)))
        weight[i] = jnp.where(four, high_half, low_half).reshape(cols, delays)
        return 0

    for n in range(CHUNKS):
        bucket_chunks[n].wait()
        lax.fori_loop(n * chunk, (n + 1) * chunk, weigh, 0)
    for load in obs_chunks:
        load.wait()

    c16[...] = fc[...].astype(bf16)
    c_mine = pl.ds(pl.multiple_of(xy * part_c, 8), part_c)

    for step in range(STEPS):
        last = step == STEPS - 1
        arrived(n_hour, a_all, step, ROWS_A)
        arrived(n_camp, b_all, step, ROWS_B)
        a32[...] = a_all[step].astype(f32).reshape(rows, rank)
        b32[...] = b_all[step].astype(f32).reshape(cols, rank)
        b16[...] = b32[...].astype(bf16)
        if step > 0:
            arrived(n_xy, c_all, step - 1, ROWS_C)
            c16[...] = c_all[step - 1].astype(f32).reshape(delays, rank).astype(bf16)
        ct16[...] = c16[...].astype(f32).T.astype(bf16)
        gb[...] = jnp.zeros_like(gb)
        gc[...] = jnp.zeros_like(gc)

        def block(t, _):
            owner = (hour + 1 + t) % n_hour
            first = owner * part_a
            for half in range(part_a // 4):
                begin = first + half * 4
                pairs = jnp.concatenate([a32[pl.ds(begin + u, 1), :].astype(bf16) * b16[...] for u in range(4)], 0)
                model = dot(pairs, ct16[...], ((1,), (0,)))
                seen = obs[pl.ds(begin, 4)].reshape(4 * cols, delays).astype(f32)
                residual = (weight[pl.ds(begin, 4)].reshape(4 * cols, delays) * (model - seen)).astype(bf16)
                spread = dot(residual, c16[...], ((1,), (0,)))
                gc[...] += dot(residual, pairs, ((0,), (0,)))
                sums = gb[...]
                for u in range(4):
                    mine = spread[u * cols : (u + 1) * cols]
                    sums = sums + a32[pl.ds(begin + u, 1), :] * mine
                    ga[pl.ds(half * 4 + u, 1), :] = jnp.sum(b32[...] * mine, axis=0, keepdims=True)
                gb[...] = sums
            piece = ga[...].astype(bf16)

            @pl.when(t < n_hour - 1)
            def _():
                ga_out[step, owner] = piece
                send(ga_out.at[step, owner], ga_in.at[step, hour], step, GRAD_A, hour_peer(owner))

            @pl.when(t == n_hour - 1)
            def _():
                ga_in[step, owner] = piece

            return 0

        lax.fori_loop(0, n_hour, block, 0)

        gc_out[step] = gc[...].reshape(gc_out.shape[1:]).astype(bf16)
        gc_in[step, xy] = gc_out[step, xy]
        to_each(by_xy, gc_out, gc_in, step, GRAD_C)
        gb_out[step] = gb[...].reshape(gb_out.shape[1:]).astype(bf16)
        gb_in[step, camp] = gb_out[step, camp]
        to_each(by_camp, gb_out, gb_in, step, GRAD_B)

        arrived(n_hour, ga_in, step, GRAD_A)
        fa[...], ma[...], va[...] = adam_update(fa[...], ma[...], va[...], total(ga_in, step, n_hour), scale_a)
        if not last:
            give(a_own, a_all, by_hour, fa[...].astype(bf16), step + 1, ROWS_A)

        arrived(n_xy, gc_in, step, GRAD_C)
        give(sc_out, sc_in, by_cz, total(gc_in, step, n_xy).astype(bf16), step, SUM_C)

        arrived(n_camp, gb_in, step, GRAD_B)
        fb[...], mb[...], vb[...] = adam_update(fb[...], mb[...], vb[...], total(gb_in, step, n_camp), scale_b)
        if not last:
            give(b_own, b_all, by_camp, fb[...].astype(bf16), step + 1, ROWS_B)

        arrived(n_cz, sc_in, step, SUM_C)
        fresh = adam_update(fc[c_mine], mc[c_mine], vc[c_mine], total(sc_in, step, n_cz), scale_c)
        fc[c_mine], mc[c_mine], vc[c_mine] = fresh
        if not last:
            give(c_own, c_all, by_xy, fresh[0].astype(bf16), step, ROWS_C)
        else:
            c_last[0, xy] = fresh[0]
            size, me, peer = by_xy

            def final(t, _):
                send(c_last.at[0, me], c_last.at[0, me], step, ROWS_C, peer((me + t) % size))
                return 0

            lax.fori_loop(1, size, final, 0)
            new_a[...] = fa[...]
            new_b[...] = fb[...]
            got = c_last.at[0, pl.ds(0, n_xy - 1)]
            pltpu.make_async_copy(got, got, recv_sem.at[step, ROWS_C]).wait()
            new_c[...] = c_last[0].reshape(delays, rank)

    def sent(size, buf, step, kind):
        gone = buf.at[step, pl.ds(0, size - 1)]
        pltpu.make_async_copy(gone, gone, send_sem.at[step, kind]).wait()

    for step in range(STEPS):
        sent(n_hour, a_all, step, ROWS_A)
        sent(n_camp, b_all, step, ROWS_B)
        sent(n_hour, ga_in, step, GRAD_A)
        sent(n_camp, gb_in, step, GRAD_B)
        sent(n_xy, gc_in, step, GRAD_C)
        sent(n_cz, sc_in, step, SUM_C)
        if step < STEPS - 1:
            sent(n_xy, c_all, step, ROWS_C)
        else:
            gone = c_last.at[0, pl.ds(0, n_xy - 1)]
            pltpu.make_async_copy(gone, gone, send_sem.at[step, ROWS_C]).wait()


def body(observed, bucket, propensity, *state):
    rows, cols, delays = observed.shape
    part_a, rank = state[0].shape
    part_b = state[3].shape[0]
    n_camp, n_hour = lax.axis_size("camp"), lax.axis_size("hour")
    sizes = split_sizes(n_camp, n_hour)
    high, along_y, cores, along_x, low = sizes
    n_xy, n_cz = along_x * along_y, cores * high * low
    part_c = delays // n_xy
    scales = (
        1.0 / math.sqrt(cols * n_hour * delays),
        1.0 / math.sqrt(rows * n_camp * delays),
        1.0 / math.sqrt(rows * n_camp * cols * n_hour),
    )
    vmem = pltpu.VMEM
    scratch = [
        vmem((rows, cols, delays), bf16),
        vmem((rows, cols, delays), jnp.int32),
        vmem((rows, cols, delays), f32),
        pltpu.SMEM(propensity.shape, f32),
        vmem((propensity.shape[0], 8, delays), f32),
    ]
    scratch += [vmem(s.shape, f32) for s in state]
    scratch += [vmem((STEPS, p, rank), bf16) for p in (part_a, part_b, part_c)]
    scratch += [
        vmem((STEPS, n_hour, part_a, rank), bf16),
        vmem((STEPS, n_camp, part_b, rank), bf16),
        vmem((STEPS, n_xy, part_c, rank), bf16),
        vmem((1, n_xy, part_c, rank), f32),
        vmem((STEPS, n_hour, part_a, rank), bf16),
        vmem((STEPS, n_camp, part_b, rank), bf16),
        vmem((STEPS, n_xy, part_c, rank), bf16),
        vmem((STEPS, part_c, rank), bf16),
        vmem((STEPS, n_hour, part_a, rank), bf16),
        vmem((STEPS, n_camp, part_b, rank), bf16),
        vmem((STEPS, n_xy, part_c, rank), bf16),
        vmem((STEPS, n_cz, part_c, rank), bf16),
        vmem((rows, rank), f32),
        vmem((cols, rank), bf16),
        vmem((cols, rank), f32),
        vmem((delays, rank), bf16),
        vmem((rank, delays), bf16),
        vmem((part_a, rank), f32),
        vmem((cols, rank), f32),
        vmem((delays, rank), f32),
        pltpu.SemaphoreType.DMA((10,)),
        pltpu.SemaphoreType.DMA((2, CHUNKS)),
        pltpu.SemaphoreType.DMA((STEPS, KINDS)),
        pltpu.SemaphoreType.DMA((STEPS, KINDS)),
    ]
    anywhere, whole = pl.BlockSpec(memory_space=pltpu.HBM), pl.BlockSpec(memory_space=vmem)
    return pl.pallas_call(
        functools.partial(kernel, sizes, scales),
        out_shape=(
            jax.ShapeDtypeStruct(state[0].shape, f32),
            jax.ShapeDtypeStruct(state[3].shape, f32),
            jax.ShapeDtypeStruct(state[6].shape, f32),
        ),
        in_specs=[anywhere] * 12,
        out_specs=(whole, whole, whole),
        scratch_shapes=scratch,
        compiler_params=pltpu.CompilerParams(
            collective_id=0, has_side_effects=True, vmem_limit_bytes=67_043_328
        ),
        name="factor_steps",
    )(observed, bucket, propensity, *state)


def solution(mesh):
    rows_camp, rows_hour = P(("camp", "hour"), None), P(("hour", "camp"), None)
    in_specs = (
        P("camp", "hour", None),
        P("camp", "hour", None),
        P(),
        rows_camp,
        rows_camp,
        rows_camp,
        rows_hour,
        rows_hour,
        rows_hour,
        P(),
        P(),
        P(),
    )
    out_specs = (rows_camp, rows_hour, P())
    return jax.shard_map(body, mesh=mesh, in_specs=in_specs, out_specs=out_specs, check_vma=False)
```

time: 265 us -> 75.6 us (0.29)
  starting transfers between devices: 79.4 us -> 0 us
  Pallas kernels: 0 us -> 70.6 us
  waiting for transfers between devices: 68.2 us -> 0 us
  matrix products: 43.4 us -> 0 us
  other arithmetic: 33.6 us -> 0 us
  local copies, waits for them, and re-layouts: 23.6 us -> 4.16 us
  blocking collectives: 13.5 us -> 0 us
    all_to_all x13 -> x0, starting transfers between devices: 79.4 us -> none  [the longest x8 45.3 us: copy_for_each(): return lax.all_to_all(copies, axis, split_axis=0, concat_axis=0, tiled=True)]
    pallas_call x0 -> x1, Pallas kernels: none -> 70.6 us  [body(): pl.pallas_call(functools.partial(kernel, sizes, scales), out_shape=(jax.S...]
    all_to_all x13 -> x0, waiting for transfers between devices: 68.2 us -> none  [the longest x8 42.6 us: copy_for_each(): return lax.all_to_all(copies, axis, split_axis=0, concat_axis=0, tiled=True)]
    dot_general x6 -> x0, matrix products: 43.4 us -> none  [the longest x2 21 us: local_terms(): lax.dot_general(camp_block, khatri, (((1,), (1,)), ((), ())), preferred_e...]
    add x1 -> x0, other arithmetic: 15.2 us -> none  [entry_weights(): weight + jnp.where(bucket == bucket_level + 1, inverse[bucket_level], jnp...]
    convert_element_type x10 -> x0, other arithmetic: 14.8 us -> none  [the longest x2 13.3 us: local_terms(): khatri = (hour_block.astype(jnp.float32)[:, None, :] * delay_block.astype...]
    all_to_all x1 -> x0, blocking collectives: 13.5 us -> none  [summed_on_arrival(): lax.all_to_all(pieces, axis, split_axis=0, concat_axis=0, tiled=True)]
    add x1 -> x0, local copies, waits for them, and re-layouts: 9.34 us -> none  [entry_weights(): weight + jnp.where(bucket == bucket_level + 1, inverse[bucket_level], jnp...]
  transfers between devices with their start and end apart: 13 -> 0, of which waited for: 11 -> 0; matrix products, arithmetic and copies ran while one was open for 25% -> 0% of each run, Pallas kernels for 0% -> 0%
where the time goes in v1:
time: 75.6 us; the launch traced here: 75.4 us
  Pallas kernels  70.6 us (93%)
  local copies, waits for them, and re-layouts  4.16 us (6%)
    pallas_call x1, Pallas kernels, body(): pl.pallas_call(functools.partial(kernel, sizes, scales), out_shape=(jax.S...  70.6 us
    unnamed x3, local copies, waits for them, and re-layouts  4.16 us

profile of v1, /device:TPU:1, one launch (start us, length us, event | category | flops | bytes accessed | tf_op | source)
XLA Modules:
  0.0 75.4 jit_solution(15361154273638483556)
XLA Ops:
  0.6 70.6 %factor_steps.1 = (f32[8,256]{1,0:T(8,128)}, f32[8,256]{1,0:T(8,128)}, f32[128,256]{1,0:T(8,128)}) custom-call(bf16[128,128,128]{2,1,0:T(8,128)(2,1)} %obs_hbm.1, s32[128,128,128]{2,1,0:T(8,128)} %bucket_hbm.1, f32[8]{0:T(128)} %prop_hbm.1, f32[8,256]{1,0:T(8,128)} %refs_0_.1, f32[8,256]{1,0:T(8,128)} %refs_1_.1, f32[8,256]{1,0:T(8,128)} %refs_2_.1, ...), custom_call_target="tpu_custom_call" | custom-call | tf_op jit(solution)/shard_map/factor_steps/pallas_call | solution.py:378
  71.3 1.3 %copy.18 = f32[8,256]{1,0:T(8,128)} copy(f32[8,256]{1,0:T(8,128)} %get-tuple-element.6) | data formatting | bytes 16384
  72.6 1.3 %copy.19 = f32[8,256]{1,0:T(8,128)} copy(f32[8,256]{1,0:T(8,128)} %get-tuple-element.7) | data formatting | bytes 16384
  73.9 1.6 %copy.20 = f32[128,256]{1,0:T(8,128)} copy(f32[128,256]{1,0:T(8,128)} %get-tuple-element.8) | data formatting | bytes 262144

commit v2 on v1

--- a/solution.py
+++ b/solution.py
@@ -20,6 +20,8 @@
 bf16 = jnp.bfloat16
 
 CHUNKS = 8
+FIRST = 32
+GROUP = 8
 ROWS_A, ROWS_B, ROWS_C, GRAD_A, GRAD_B, GRAD_C, SUM_C = range(7)
 KINDS = 7
 
@@ -59,6 +61,7 @@
         weight,
         prop,
         inverse,
+        resid,
         fa,
         ma,
         va,
@@ -88,8 +91,7 @@
         b32,
         c16,
         ct16,
-        ga,
-        gb,
+        ga8,
         gc,
         state_sem,
         chunk_sem,
@@ -102,11 +104,13 @@
     scale_a, scale_b, scale_c = scales
     rows, cols, delays = obs.shape
     rank = a32.shape[1]
-    part_a, part_c = rows // n_hour, delays // n_xy
+    part_b, part_c = cols // n_camp, delays // n_xy
+    width = cores * part_b
 
     camp, hour = lax.axis_index("camp"), lax.axis_index("hour")
-    z_hi, y, core = camp // (along_y * cores), (camp // cores) % along_y, camp % cores
-    x, z_lo = hour // low, hour % low
+    div, rem = lax.div, lax.rem
+    z_hi, y, core = div(camp, along_y * cores), rem(div(camp, cores), along_y), rem(camp, cores)
+    x, z_lo = div(hour, low), rem(hour, low)
     xy = x * along_y + y
     cz = (core * high + z_hi) * low + z_lo
 
@@ -117,11 +121,11 @@
         return {"camp": p, "hour": hour}
 
     def xy_peer(p):
-        return {"camp": (z_hi * along_y + p % along_y) * cores + core, "hour": (p // along_y) * low + z_lo}
+        return {"camp": (z_hi * along_y + rem(p, along_y)) * cores + core, "hour": div(p, along_y) * low + z_lo}
 
     def cz_peer(p):
-        at = (p // low) % high
-        return {"camp": (at * along_y + y) * cores + p // (low * high), "hour": x * low + p % low}
+        at = rem(div(p, low), high)
+        return {"camp": (at * along_y + y) * cores + div(p, low * high), "hour": x * low + rem(p, low)}
 
     by_hour = (n_hour, hour, hour_peer)
     by_camp = (n_camp, camp, camp_peer)
@@ -146,12 +150,8 @@
 
     barrier = pltpu.get_barrier_semaphore()
     for size, me, peer in groups:
-
-        def greet(t, _, size=size, me=me, peer=peer):
-            pl.semaphore_signal(barrier, inc=1, device_id=peer((me + t) % size), device_id_type=MESH)
-            return 0
-
-        lax.fori_loop(1, size, greet, 0)
+        for t in range(1, size):
+            pl.semaphore_signal(barrier, inc=1, device_id=peer(rem(me + t, size)), device_id_type=MESH)
     pl.semaphore_wait(barrier, sum(size - 1 for size, _, _ in groups))
 
     def send(src, dst, step, kind, device):
@@ -166,14 +166,10 @@
 
     def to_each(group, src, dst, step, kind):
         size, me, peer = group
-
-        def one(t, _):
-            p = (me + t) % size
+        for t in range(1, size):
+            p = rem(me + t, size)
             block = src.at[step] if len(src.shape) == len(dst.shape) - 1 else src.at[step, p]
             send(block, dst.at[step, me], step, kind, peer(p))
-            return 0
-
-        lax.fori_loop(1, size, one, 0)
 
     def arrived(size, dst, step, kind):
         got = dst.at[step, pl.ds(0, size - 1)]
@@ -231,60 +227,78 @@
             arrived(n_xy, c_all, step - 1, ROWS_C)
             c16[...] = c_all[step - 1].astype(f32).reshape(delays, rank).astype(bf16)
         ct16[...] = c16[...].astype(f32).T.astype(bf16)
-        gb[...] = jnp.zeros_like(gb)
+        ga8[...] = jnp.zeros_like(ga8)
         gc[...] = jnp.zeros_like(gc)
 
-        def block(t, _):
-            owner = (hour + 1 + t) % n_hour
-            first = owner * part_a
-            for half in range(part_a // 4):
-                begin = first + half * 4
-                pairs = jnp.concatenate([a32[pl.ds(begin + u, 1), :].astype(bf16) * b16[...] for u in range(4)], 0)
-                model = dot(pairs, ct16[...], ((1,), (0,)))
-                seen = obs[pl.ds(begin, 4)].reshape(4 * cols, delays).astype(f32)
-                residual = (weight[pl.ds(begin, 4)].reshape(4 * cols, delays) * (model - seen)).astype(bf16)
-                spread = dot(residual, c16[...], ((1,), (0,)))
-                gc[...] += dot(residual, pairs, ((0,), (0,)))
-                sums = gb[...]
-                for u in range(4):
-                    mine = spread[u * cols : (u + 1) * cols]
-                    sums = sums + a32[pl.ds(begin + u, 1), :] * mine
-                    ga[pl.ds(half * 4 + u, 1), :] = jnp.sum(b32[...] * mine, axis=0, keepdims=True)
-                gb[...] = sums
-            piece = ga[...].astype(bf16)
-
-            @pl.when(t < n_hour - 1)
-            def _():
-                ga_out[step, owner] = piece
-                send(ga_out.at[step, owner], ga_in.at[step, hour], step, GRAD_A, hour_peer(owner))
-
-            @pl.when(t == n_hour - 1)
-            def _():
-                ga_in[step, owner] = piece
-
+        def first_pass(g, _):
+            begin = g * FIRST
+            pairs, residuals = [], []
+            for i in range(0, FIRST, 2):
+                at = pl.ds(begin + i, 2)
+                pair = jnp.concatenate([a32[pl.ds(begin + i + u, 1), :].astype(bf16) * b16[...] for u in range(2)], 0)
+                model = dot(pair, ct16[...], ((1,), (0,)))
+                seen = obs[at].reshape(2 * cols, delays).astype(f32)
+                residual = (weight[at].reshape(2 * cols, delays) * (model - seen)).astype(bf16)
+                resid[at] = residual.reshape(2, cols, delays)
+                pairs.append(pair)
+                residuals.append(residual)
+            gc[...] += dot(jnp.concatenate(residuals, 0), jnp.concatenate(pairs, 0), ((0,), (0,)))
             return 0
 
-        lax.fori_loop(0, n_hour, block, 0)
-
+        lax.fori_loop(0, rows // FIRST, first_pass, 0)
         gc_out[step] = gc[...].reshape(gc_out.shape[1:]).astype(bf16)
         gc_in[step, xy] = gc_out[step, xy]
         to_each(by_xy, gc_out, gc_in, step, GRAD_C)
-        gb_out[step] = gb[...].reshape(gb_out.shape[1:]).astype(bf16)
-        gb_in[step, camp] = gb_out[step, camp]
-        to_each(by_camp, gb_out, gb_in, step, GRAD_B)
+
+        def second_pass(t, _):
+            there = rem(z_hi + 1 + div(t, along_y), high) * along_y + rem(y + 1 + rem(t, along_y), along_y)
+            cut = pl.multiple_of(there * width, width)
+            at = pl.ds(cut, width)
+            sums = [jnp.zeros((8, rank), f32) for _ in range(width // 8)]
+            factor = b32[at]
+            for begin in range(0, rows, GROUP):
+                spread = dot(resid[pl.ds(begin, GROUP), at].reshape(GROUP * width, delays), c16[...], ((1,), (0,)))
+                for u in range(GROUP):
+                    row = a32[pl.ds(begin + u, 1), :]
+                    part = None
+                    for n in range(width // 8):
+                        piece = spread[u * width + n * 8 : u * width + n * 8 + 8]
+                        sums[n] = sums[n] + row * piece
+                        scaled = factor[n * 8 : n * 8 + 8] * piece
+                        part = scaled if part is None else part + scaled
+                    ga8[begin + u] += part
+            peer_rows = jnp.concatenate(sums, 0).reshape(cores, part_b, rank).astype(bf16)
+            for n in range(cores):
+                owner = there * cores + n
+
+                @pl.when(owner != camp)
+                def _(n=n, owner=owner):
+                    gb_out[step, owner] = peer_rows[n]
+                    send(gb_out.at[step, owner], gb_in.at[step, camp], step, GRAD_B, camp_peer(owner))
+
+                @pl.when(owner == camp)
+                def _(n=n, owner=owner):
+                    gb_in[step, owner] = peer_rows[n]
+
+            return 0
+
+        lax.fori_loop(0, cols // width, second_pass, 0)
+        ga_out[step] = jnp.sum(ga8[...], axis=1).reshape(ga_out.shape[1:]).astype(bf16)
+        ga_in[step, hour] = ga_out[step, hour]
+        to_each(by_hour, ga_out, ga_in, step, GRAD_A)
+
+        arrived(n_xy, gc_in, step, GRAD_C)
+        give(sc_out, sc_in, by_cz, total(gc_in, step, n_xy).astype(bf16), step, SUM_C)
+
+        arrived(n_camp, gb_in, step, GRAD_B)
+        fb[...], mb[...], vb[...] = adam_update(fb[...], mb[...], vb[...], total(gb_in, step, n_camp), scale_b)
+        if not last:
+            give(b_own, b_all, by_camp, fb[...].astype(bf16), step + 1, ROWS_B)
 
         arrived(n_hour, ga_in, step, GRAD_A)
         fa[...], ma[...], va[...] = adam_update(fa[...], ma[...], va[...], total(ga_in, step, n_hour), scale_a)
         if not last:
             give(a_own, a_all, by_hour, fa[...].astype(bf16), step + 1, ROWS_A)
-
-        arrived(n_xy, gc_in, step, GRAD_C)
-        give(sc_out, sc_in, by_cz, total(gc_in, step, n_xy).astype(bf16), step, SUM_C)
-
-        arrived(n_camp, gb_in, step, GRAD_B)
-        fb[...], mb[...], vb[...] = adam_update(fb[...], mb[...], vb[...], total(gb_in, step, n_camp), scale_b)
-        if not last:
-            give(b_own, b_all, by_camp, fb[...].astype(bf16), step + 1, ROWS_B)
 
         arrived(n_cz, sc_in, step, SUM_C)
         fresh = adam_update(fc[c_mine], mc[c_mine], vc[c_mine], total(sc_in, step, n_cz), scale_c)
@@ -293,13 +307,8 @@
             give(c_own, c_all, by_xy, fresh[0].astype(bf16), step, ROWS_C)
         else:
             c_last[0, xy] = fresh[0]
-            size, me, peer = by_xy
-
-            def final(t, _):
-                send(c_last.at[0, me], c_last.at[0, me], step, ROWS_C, peer((me + t) % size))
-                return 0
-
-            lax.fori_loop(1, size, final, 0)
+            for t in range(1, n_xy):
+                send(c_last.at[0, xy], c_last.at[0, xy], step, ROWS_C, xy_peer(rem(xy + t, n_xy)))
             new_a[...] = fa[...]
             new_b[...] = fb[...]
             got = c_last.at[0, pl.ds(0, n_xy - 1)]
@@ -345,6 +354,7 @@
         vmem((rows, cols, delays), f32),
         pltpu.SMEM(propensity.shape, f32),
         vmem((propensity.shape[0], 8, delays), f32),
+        vmem((rows, cols, delays), bf16),
     ]
     scratch += [vmem(s.shape, f32) for s in state]
     scratch += [vmem((STEPS, p, rank), bf16) for p in (part_a, part_b, part_c)]
@@ -366,30 +376,44 @@
         vmem((cols, rank), f32),
         vmem((delays, rank), bf16),
         vmem((rank, delays), bf16),
-        vmem((part_a, rank), f32),
-        vmem((cols, rank), f32),
+        vmem((rows, 8, rank), f32),
         vmem((delays, rank), f32),
         pltpu.SemaphoreType.DMA((10,)),
         pltpu.SemaphoreType.DMA((2, CHUNKS)),
         pltpu.SemaphoreType.DMA((STEPS, KINDS)),
         pltpu.SemaphoreType.DMA((STEPS, KINDS)),
     ]
+    def finish(*refs):
+        copies = [pltpu.make_async_copy(refs[i], refs[3 + i], refs[6].at[i]) for i in range(3)]
+        for c in copies:
+            c.start()
+        for c in copies:
+            c.wait()
+
     anywhere, whole = pl.BlockSpec(memory_space=pltpu.HBM), pl.BlockSpec(memory_space=vmem)
-    return pl.pallas_call(
+    made = pl.pallas_call(
         functools.partial(kernel, sizes, scales),
         out_shape=(
-            jax.ShapeDtypeStruct(state[0].shape, f32),
-            jax.ShapeDtypeStruct(state[3].shape, f32),
-            jax.ShapeDtypeStruct(state[6].shape, f32),
+            vmem(state[0].shape, f32),
+            vmem(state[3].shape, f32),
+            vmem(state[6].shape, f32),
         ),
         in_specs=[anywhere] * 12,
         out_specs=(whole, whole, whole),
         scratch_shapes=scratch,
         compiler_params=pltpu.CompilerParams(
-            collective_id=0, has_side_effects=True, vmem_limit_bytes=67_043_328
+            collective_id=0, has_side_effects=True, vmem_limit_bytes=40 * 1024 * 1024
         ),
         name="factor_steps",
-    )(observed, bucket, propensity, *state)
+    )(*[pltpu.with_memory_space_constraint(a, pltpu.HBM) for a in (observed, bucket, propensity, *state)])
+    return pl.pallas_call(
+        finish,
+        out_shape=tuple(jax.ShapeDtypeStruct(m.shape, f32) for m in made),
+        in_specs=[pl.BlockSpec(memory_space=vmem)] * 3,
+        out_specs=(pl.BlockSpec(memory_space=pl.ANY),) * 3,
+        scratch_shapes=[pltpu.SemaphoreType.DMA((3,))],
+        name="outputs",
+    )(*[pltpu.with_memory_space_constraint(m, vmem) for m in made])
 
 
 def solution(mesh):

time: 75.6 us -> 60 us (0.79)
  Pallas kernels: 70.6 us -> 59.3 us
  local copies, waits for them, and re-layouts: 4.16 us -> 0 us
    pallas_call x1 -> x2, Pallas kernels: 70.6 us -> 59.3 us  [the longest x1 58.6 us: body(): pl.pallas_call(functools.partial(kernel, sizes, scales), out_shape=(vmem(...]
    unnamed x3 -> x0, local copies, waits for them, and re-layouts: 4.16 us -> none
where the time goes in v2:
time: 60 us
  Pallas kernels  59.3 us (99%)
  between operations  0.64 us (1%)
    pallas_call x1, Pallas kernels, body(): pl.pallas_call(functools.partial(kernel, sizes, scales), out_shape=(vmem(...  58.6 us

profile of v2, /device:TPU:1, one launch (start us, length us, event | category | flops | bytes accessed | tf_op | source)
XLA Modules:
  0.0 60.0 jit_solution(7135231416020338350)
XLA Ops:
  0.6 58.6 %factor_steps.1 = (f32[8,256]{1,0:T(8,128)S(1)}, f32[8,256]{1,0:T(8,128)S(1)}, f32[128,256]{1,0:T(8,128)S(1)}) custom-call(bf16[128,128,128]{2,1,0:T(8,128)(2,1)} %obs_hbm.1, s32[128,128,128]{2,1,0:T(8,128)} %bucket_hbm.1, f32[8]{0:T(128)} %prop_hbm.1, f32[8,256]{1,0:T(8,128)} %refs_0_.1, f32[8,256]{1,0:T(8,128)} %refs_1_.1, f32[8,256]{1,0:T(8,128)} %refs_2_.1, ...), custom_call_target="tpu_custom_call" | custom-call | tf_op jit(solution)/shard_map/factor_steps/pallas_call | solution.py:394
  59.3 0.7 %outputs.1 = (f32[8,256]{1,0:T(8,128)}, f32[8,256]{1,0:T(8,128)}, f32[128,256]{1,0:T(8,128)}) custom-call(f32[8,256]{1,0:T(8,128)S(1)} %get-tuple-element.6.refs_0_, f32[8,256]{1,0:T(8,128)S(1)} %get-tuple-element.7.refs_1_, f32[128,256]{1,0:T(8,128)S(1)} %get-tuple-element.8.refs_2_), custom_call_target="tpu_custom_call" | custom-call | tf_op jit(solution)/shard_map/outputs/pallas_call | solution.py:409

commit v3 on v2

--- a/solution.py
+++ b/solution.py
@@ -20,8 +20,9 @@
 bf16 = jnp.bfloat16
 
 CHUNKS = 8
-FIRST = 32
+FIRST = 64
 GROUP = 8
+ALONG_Y = 2
 ROWS_A, ROWS_B, ROWS_C, GRAD_A, GRAD_B, GRAD_C, SUM_C = range(7)
 KINDS = 7
 
@@ -100,19 +101,21 @@
     ) = refs
     high, along_y, cores, along_x, low = sizes
     n_hour, n_camp = along_x * low, high * along_y * cores
-    n_xy, n_cz = along_x * along_y, cores * high * low
+    n_xy, n_z = along_x * along_y, high * low
+    n_cxy, half = cores * n_xy, a32.shape[1] // cores
     scale_a, scale_b, scale_c = scales
     rows, cols, delays = obs.shape
     rank = a32.shape[1]
     part_b, part_c = cols // n_camp, delays // n_xy
-    width = cores * part_b
+    owners = ALONG_Y * cores
+    width, y_blocks = owners * part_b, along_y // ALONG_Y
 
     camp, hour = lax.axis_index("camp"), lax.axis_index("hour")
     div, rem = lax.div, lax.rem
     z_hi, y, core = div(camp, along_y * cores), rem(div(camp, cores), along_y), rem(camp, cores)
     x, z_lo = div(hour, low), rem(hour, low)
     xy = x * along_y + y
-    cz = (core * high + z_hi) * low + z_lo
+    cxy, z = core * n_xy + xy, z_hi * low + z_lo
 
     def hour_peer(p):
         return {"camp": camp, "hour": p}
@@ -120,18 +123,23 @@
     def camp_peer(p):
         return {"camp": p, "hour": hour}
 
-    def xy_peer(p):
-        return {"camp": (z_hi * along_y + rem(p, along_y)) * cores + core, "hour": div(p, along_y) * low + z_lo}
-
-    def cz_peer(p):
-        at = rem(div(p, low), high)
-        return {"camp": (at * along_y + y) * cores + div(p, low * high), "hour": x * low + rem(p, low)}
+    def cxy_peer(p):
+        at = rem(p, n_xy)
+        return {"camp": (z_hi * along_y + rem(at, along_y)) * cores + div(p, n_xy), "hour": div(at, along_y) * low + z_lo}
+
+    def z_peer(p):
+        return {"camp": (div(p, low) * along_y + y) * cores + core, "hour": x * low + rem(p, low)}
 
     by_hour = (n_hour, hour, hour_peer)
     by_camp = (n_camp, camp, camp_peer)
-    by_xy = (n_xy, xy, xy_peer)
-    by_cz = (n_cz, cz, cz_peer)
-    groups = (by_hour, by_camp, by_xy, by_cz)
+    by_cxy = (n_cxy, cxy, cxy_peer)
+    by_z = (n_z, z, z_peer)
+    groups = (by_camp, by_hour, by_cxy, by_z)
+
+    barrier = pltpu.get_barrier_semaphore()
+    for size, me, peer in groups:
+        for t in range(1, size):
+            pl.semaphore_signal(barrier, inc=1, device_id=peer(rem(me + t, size)), device_id_type=MESH)
 
     states = (fa, ma, va, fb, mb, vb, fc, mc, vc)
     loads = [pltpu.make_async_copy(h, v, state_sem.at[i]) for i, (h, v) in enumerate(zip(state_hbm, states))]
@@ -148,10 +156,6 @@
     for load in bucket_chunks + obs_chunks:
         load.start()
 
-    barrier = pltpu.get_barrier_semaphore()
-    for size, me, peer in groups:
-        for t in range(1, size):
-            pl.semaphore_signal(barrier, inc=1, device_id=peer(rem(me + t, size)), device_id_type=MESH)
     pl.semaphore_wait(barrier, sum(size - 1 for size, _, _ in groups))
 
     def send(src, dst, step, kind, device):
@@ -214,21 +218,26 @@
         load.wait()
 
     c16[...] = fc[...].astype(bf16)
-    c_mine = pl.ds(pl.multiple_of(xy * part_c, 8), part_c)
+    c_mine = (pl.ds(pl.multiple_of(xy * part_c, 8), part_c), pl.ds(pl.multiple_of(core * half, 128), half))
+
+    def halves(buf):
+        return [(buf.at[pl.ds(n * n_xy, n_xy)], slice(n * half, (n + 1) * half)) for n in range(cores)]
+
 
     for step in range(STEPS):
         last = step == STEPS - 1
+        ga8[...] = jnp.zeros_like(ga8)
+        gc[...] = jnp.zeros_like(gc)
         arrived(n_hour, a_all, step, ROWS_A)
         arrived(n_camp, b_all, step, ROWS_B)
         a32[...] = a_all[step].astype(f32).reshape(rows, rank)
         b32[...] = b_all[step].astype(f32).reshape(cols, rank)
         b16[...] = b32[...].astype(bf16)
         if step > 0:
-            arrived(n_xy, c_all, step - 1, ROWS_C)
-            c16[...] = c_all[step - 1].astype(f32).reshape(delays, rank).astype(bf16)
+            arrived(n_cxy, c_all, step - 1, ROWS_C)
+            for blocks, ranks in halves(c_all.at[step - 1]):
+                c16[:, ranks] = blocks[...].astype(f32).reshape(delays, half).astype(bf16)
         ct16[...] = c16[...].astype(f32).T.astype(bf16)
-        ga8[...] = jnp.zeros_like(ga8)
-        gc[...] = jnp.zeros_like(gc)
 
         def first_pass(g, _):
             begin = g * FIRST
@@ -246,12 +255,14 @@
             return 0
 
         lax.fori_loop(0, rows // FIRST, first_pass, 0)
-        gc_out[step] = gc[...].reshape(gc_out.shape[1:]).astype(bf16)
-        gc_in[step, xy] = gc_out[step, xy]
-        to_each(by_xy, gc_out, gc_in, step, GRAD_C)
+        for blocks, ranks in halves(gc_out.at[step]):
+            blocks[...] = gc[:, ranks].reshape(n_xy, part_c, half).astype(bf16)
+        gc_in[step, cxy] = gc_out[step, cxy]
+        to_each(by_cxy, gc_out, gc_in, step, GRAD_C)
 
         def second_pass(t, _):
-            there = rem(z_hi + 1 + div(t, along_y), high) * along_y + rem(y + 1 + rem(t, along_y), along_y)
+            there = rem(z_hi + 1 + div(t, y_blocks), high) * y_blocks
+            there += rem(div(y, ALONG_Y) + 1 + rem(t, y_blocks), y_blocks)
             cut = pl.multiple_of(there * width, width)
             at = pl.ds(cut, width)
             sums = [jnp.zeros((8, rank), f32) for _ in range(width // 8)]
@@ -267,9 +278,9 @@
                         scaled = factor[n * 8 : n * 8 + 8] * piece
                         part = scaled if part is None else part + scaled
                     ga8[begin + u] += part
-            peer_rows = jnp.concatenate(sums, 0).reshape(cores, part_b, rank).astype(bf16)
-            for n in range(cores):
-                owner = there * cores + n
+            peer_rows = jnp.concatenate(sums, 0).reshape(owners, part_b, rank).astype(bf16)
+            for n in range(owners):
+                owner = there * owners + n
 
                 @pl.when(owner != camp)
                 def _(n=n, owner=owner):
@@ -283,37 +294,38 @@
             return 0
 
         lax.fori_loop(0, cols // width, second_pass, 0)
+        arrived(n_cxy, gc_in, step, GRAD_C)
+        give(sc_out, sc_in, by_z, total(gc_in, step, n_cxy).astype(bf16), step, SUM_C)
         ga_out[step] = jnp.sum(ga8[...], axis=1).reshape(ga_out.shape[1:]).astype(bf16)
         ga_in[step, hour] = ga_out[step, hour]
         to_each(by_hour, ga_out, ga_in, step, GRAD_A)
-
-        arrived(n_xy, gc_in, step, GRAD_C)
-        give(sc_out, sc_in, by_cz, total(gc_in, step, n_xy).astype(bf16), step, SUM_C)
 
         arrived(n_camp, gb_in, step, GRAD_B)
         fb[...], mb[...], vb[...] = adam_update(fb[...], mb[...], vb[...], total(gb_in, step, n_camp), scale_b)
         if not last:
             give(b_own, b_all, by_camp, fb[...].astype(bf16), step + 1, ROWS_B)
 
+        arrived(n_z, sc_in, step, SUM_C)
+        fresh = adam_update(fc[c_mine], mc[c_mine], vc[c_mine], total(sc_in, step, n_z), scale_c)
+        fc[c_mine], mc[c_mine], vc[c_mine] = fresh
+        if not last:
+            give(c_own, c_all, by_cxy, fresh[0].astype(bf16), step, ROWS_C)
+        else:
+            c_last[0, cxy] = fresh[0]
+            for t in range(1, n_cxy):
+                send(c_last.at[0, cxy], c_last.at[0, cxy], step, ROWS_C, cxy_peer(rem(cxy + t, n_cxy)))
+
         arrived(n_hour, ga_in, step, GRAD_A)
         fa[...], ma[...], va[...] = adam_update(fa[...], ma[...], va[...], total(ga_in, step, n_hour), scale_a)
         if not last:
             give(a_own, a_all, by_hour, fa[...].astype(bf16), step + 1, ROWS_A)
-
-        arrived(n_cz, sc_in, step, SUM_C)
-        fresh = adam_update(fc[c_mine], mc[c_mine], vc[c_mine], total(sc_in, step, n_cz), scale_c)
-        fc[c_mine], mc[c_mine], vc[c_mine] = fresh
-        if not last:
-            give(c_own, c_all, by_xy, fresh[0].astype(bf16), step, ROWS_C)
         else:
-            c_last[0, xy] = fresh[0]
-            for t in range(1, n_xy):
-                send(c_last.at[0, xy], c_last.at[0, xy], step, ROWS_C, xy_peer(rem(xy + t, n_xy)))
             new_a[...] = fa[...]
             new_b[...] = fb[...]
-            got = c_last.at[0, pl.ds(0, n_xy - 1)]
+            got = c_last.at[0, pl.ds(0, n_cxy - 1)]
             pltpu.make_async_copy(got, got, recv_sem.at[step, ROWS_C]).wait()
-            new_c[...] = c_last[0].reshape(delays, rank)
+            for blocks, ranks in halves(c_last.at[0]):
+                new_c[:, ranks] = blocks[...].reshape(delays, half)
 
     def sent(size, buf, step, kind):
         gone = buf.at[step, pl.ds(0, size - 1)]
@@ -324,12 +336,12 @@
         sent(n_camp, b_all, step, ROWS_B)
         sent(n_hour, ga_in, step, GRAD_A)
         sent(n_camp, gb_in, step, GRAD_B)
-        sent(n_xy, gc_in, step, GRAD_C)
-        sent(n_cz, sc_in, step, SUM_C)
+        sent(n_cxy, gc_in, step, GRAD_C)
+        sent(n_z, sc_in, step, SUM_C)
         if step < STEPS - 1:
-            sent(n_xy, c_all, step, ROWS_C)
+            sent(n_cxy, c_all, step, ROWS_C)
         else:
-            gone = c_last.at[0, pl.ds(0, n_xy - 1)]
+            gone = c_last.at[0, pl.ds(0, n_cxy - 1)]
             pltpu.make_async_copy(gone, gone, send_sem.at[step, ROWS_C]).wait()
 
 
@@ -340,8 +352,8 @@
     n_camp, n_hour = lax.axis_size("camp"), lax.axis_size("hour")
     sizes = split_sizes(n_camp, n_hour)
     high, along_y, cores, along_x, low = sizes
-    n_xy, n_cz = along_x * along_y, cores * high * low
-    part_c = delays // n_xy
+    n_xy, n_z = along_x * along_y, high * low
+    n_cxy, half, part_c = cores * n_xy, rank // cores, delays // n_xy
     scales = (
         1.0 / math.sqrt(cols * n_hour * delays),
         1.0 / math.sqrt(rows * n_camp * delays),
@@ -357,20 +369,20 @@
         vmem((rows, cols, delays), bf16),
     ]
     scratch += [vmem(s.shape, f32) for s in state]
-    scratch += [vmem((STEPS, p, rank), bf16) for p in (part_a, part_b, part_c)]
+    scratch += [vmem((STEPS, *p), bf16) for p in ((part_a, rank), (part_b, rank), (part_c, half))]
     scratch += [
         vmem((STEPS, n_hour, part_a, rank), bf16),
         vmem((STEPS, n_camp, part_b, rank), bf16),
-        vmem((STEPS, n_xy, part_c, rank), bf16),
-        vmem((1, n_xy, part_c, rank), f32),
+        vmem((STEPS, n_cxy, part_c, half), bf16),
+        vmem((1, n_cxy, part_c, half), f32),
         vmem((STEPS, n_hour, part_a, rank), bf16),
         vmem((STEPS, n_camp, part_b, rank), bf16),
-        vmem((STEPS, n_xy, part_c, rank), bf16),
-        vmem((STEPS, part_c, rank), bf16),
+        vmem((STEPS, n_cxy, part_c, half), bf16),
+        vmem((STEPS, part_c, half), bf16),
         vmem((STEPS, n_hour, part_a, rank), bf16),
         vmem((STEPS, n_camp, part_b, rank), bf16),
-        vmem((STEPS, n_xy, part_c, rank), bf16),
-        vmem((STEPS, n_cz, part_c, rank), bf16),
+        vmem((STEPS, n_cxy, part_c, half), bf16),
+        vmem((STEPS, n_z, part_c, half), bf16),
         vmem((rows, rank), f32),
         vmem((cols, rank), bf16),
         vmem((cols, rank), f32),

time: 60 us -> 58.9 us (0.982)
  Pallas kernels: 59.3 us -> 58.2 us
    pallas_call x1, Pallas kernels: 58.6 us -> 57.5 us  [body(): pl.pallas_call(functools.partial(kernel, sizes, scales), out_shape=(vmem(...]
where the time goes in v3:
time: 58.9 us; the launch traced here: 58.8 us
  Pallas kernels  58.2 us (99%)
  between operations  0.64 us (1%)
    pallas_call x1, Pallas kernels, body(): pl.pallas_call(functools.partial(kernel, sizes, scales), out_shape=(vmem(...  57.5 us

profile of v3, /device:TPU:1, one launch (start us, length us, event | category | flops | bytes accessed | tf_op | source)
XLA Modules:
  0.0 58.8 jit_solution(8795185278537824237)
XLA Ops:
  0.6 57.5 %factor_steps.1 = (f32[8,256]{1,0:T(8,128)S(1)}, f32[8,256]{1,0:T(8,128)S(1)}, f32[128,256]{1,0:T(8,128)S(1)}) custom-call(bf16[128,128,128]{2,1,0:T(8,128)(2,1)} %obs_hbm.1, s32[128,128,128]{2,1,0:T(8,128)} %bucket_hbm.1, f32[8]{0:T(128)} %prop_hbm.1, f32[8,256]{1,0:T(8,128)} %refs_0_.1, f32[8,256]{1,0:T(8,128)} %refs_1_.1, f32[8,256]{1,0:T(8,128)} %refs_2_.1, ...), custom_call_target="tpu_custom_call" | custom-call | tf_op jit(solution)/shard_map/factor_steps/pallas_call | solution.py:406
  58.1 0.7 %outputs.1 = (f32[8,256]{1,0:T(8,128)}, f32[8,256]{1,0:T(8,128)}, f32[128,256]{1,0:T(8,128)}) custom-call(f32[8,256]{1,0:T(8,128)S(1)} %get-tuple-element.6.refs_0_, f32[8,256]{1,0:T(8,128)S(1)} %get-tuple-element.7.refs_1_, f32[128,256]{1,0:T(8,128)S(1)} %get-tuple-element.8.refs_2_), custom_call_target="tpu_custom_call" | custom-call | tf_op jit(solution)/shard_map/outputs/pallas_call | solution.py:421

commit v4 on v3

--- a/solution.py
+++ b/solution.py
@@ -134,12 +134,7 @@
     by_camp = (n_camp, camp, camp_peer)
     by_cxy = (n_cxy, cxy, cxy_peer)
     by_z = (n_z, z, z_peer)
-    groups = (by_camp, by_hour, by_cxy, by_z)
-
-    barrier = pltpu.get_barrier_semaphore()
-    for size, me, peer in groups:
-        for t in range(1, size):
-            pl.semaphore_signal(barrier, inc=1, device_id=peer(rem(me + t, size)), device_id_type=MESH)
+    groups = (by_hour, by_camp, by_cxy, by_z)
 
     states = (fa, ma, va, fb, mb, vb, fc, mc, vc)
     loads = [pltpu.make_async_copy(h, v, state_sem.at[i]) for i, (h, v) in enumerate(zip(state_hbm, states))]
@@ -156,6 +151,10 @@
     for load in bucket_chunks + obs_chunks:
         load.start()
 
+    barrier = pltpu.get_barrier_semaphore()
+    for size, me, peer in groups:
+        for t in range(1, size):
+            pl.semaphore_signal(barrier, inc=1, device_id=peer(rem(me + t, size)), device_id_type=MESH)
     pl.semaphore_wait(barrier, sum(size - 1 for size, _, _ in groups))
 
     def send(src, dst, step, kind, device):
@@ -294,16 +293,22 @@
             return 0
 
         lax.fori_loop(0, cols // width, second_pass, 0)
-        arrived(n_cxy, gc_in, step, GRAD_C)
-        give(sc_out, sc_in, by_z, total(gc_in, step, n_cxy).astype(bf16), step, SUM_C)
         ga_out[step] = jnp.sum(ga8[...], axis=1).reshape(ga_out.shape[1:]).astype(bf16)
         ga_in[step, hour] = ga_out[step, hour]
         to_each(by_hour, ga_out, ga_in, step, GRAD_A)
+
+        arrived(n_cxy, gc_in, step, GRAD_C)
+        give(sc_out, sc_in, by_z, total(gc_in, step, n_cxy).astype(bf16), step, SUM_C)
 
         arrived(n_camp, gb_in, step, GRAD_B)
         fb[...], mb[...], vb[...] = adam_update(fb[...], mb[...], vb[...], total(gb_in, step, n_camp), scale_b)
         if not last:
             give(b_own, b_all, by_camp, fb[...].astype(bf16), step + 1, ROWS_B)
+
+        arrived(n_hour, ga_in, step, GRAD_A)
+        fa[...], ma[...], va[...] = adam_update(fa[...], ma[...], va[...], total(ga_in, step, n_hour), scale_a)
+        if not last:
+            give(a_own, a_all, by_hour, fa[...].astype(bf16), step + 1, ROWS_A)
 
         arrived(n_z, sc_in, step, SUM_C)
         fresh = adam_update(fc[c_mine], mc[c_mine], vc[c_mine], total(sc_in, step, n_z), scale_c)
@@ -314,12 +319,6 @@
             c_last[0, cxy] = fresh[0]
             for t in range(1, n_cxy):
                 send(c_last.at[0, cxy], c_last.at[0, cxy], step, ROWS_C, cxy_peer(rem(cxy + t, n_cxy)))
-
-        arrived(n_hour, ga_in, step, GRAD_A)
-        fa[...], ma[...], va[...] = adam_update(fa[...], ma[...], va[...], total(ga_in, step, n_hour), scale_a)
-        if not last:
-            give(a_own, a_all, by_hour, fa[...].astype(bf16), step + 1, ROWS_A)
-        else:
             new_a[...] = fa[...]
             new_b[...] = fb[...]
             got = c_last.at[0, pl.ds(0, n_cxy - 1)]

time: 58.9 us -> 57.8 us (0.981)
  Pallas kernels: 58.2 us -> 57.1 us
    pallas_call x1, Pallas kernels: 57.5 us -> 56.4 us  [body(): pl.pallas_call(functools.partial(kernel, sizes, scales), out_shape=(vmem(...]
where the time goes in v4:
time: 57.8 us; the launch traced here: 57.7 us
  Pallas kernels  57.1 us (99%)
  between operations  0.64 us (1%)
    pallas_call x1, Pallas kernels, body(): pl.pallas_call(functools.partial(kernel, sizes, scales), out_shape=(vmem(...  56.4 us

profile of v4, /device:TPU:1, one launch (start us, length us, event | category | flops | bytes accessed | tf_op | source)
XLA Modules:
  0.0 57.7 jit_solution(2553651112477987045)
XLA Ops:
  0.6 56.4 %factor_steps.1 = (f32[8,256]{1,0:T(8,128)S(1)}, f32[8,256]{1,0:T(8,128)S(1)}, f32[128,256]{1,0:T(8,128)S(1)}) custom-call(bf16[128,128,128]{2,1,0:T(8,128)(2,1)} %obs_hbm.1, s32[128,128,128]{2,1,0:T(8,128)} %bucket_hbm.1, f32[8]{0:T(128)} %prop_hbm.1, f32[8,256]{1,0:T(8,128)} %refs_0_.1, f32[8,256]{1,0:T(8,128)} %refs_1_.1, f32[8,256]{1,0:T(8,128)} %refs_2_.1, ...), custom_call_target="tpu_custom_call" | custom-call | tf_op jit(solution)/shard_map/factor_steps/pallas_call | solution.py:405
  57.0 0.7 %outputs.1 = (f32[8,256]{1,0:T(8,128)}, f32[8,256]{1,0:T(8,128)}, f32[128,256]{1,0:T(8,128)}) custom-call(f32[8,256]{1,0:T(8,128)S(1)} %get-tuple-element.6.refs_0_, f32[8,256]{1,0:T(8,128)S(1)} %get-tuple-element.7.refs_1_, f32[128,256]{1,0:T(8,128)S(1)} %get-tuple-element.8.refs_2_), custom_call_target="tpu_custom_call" | custom-call | tf_op jit(solution)/shard_map/outputs/pallas_call | solution.py:420
